TPU v7x, 32 devices: a whole 2x2x4 slice. The times are simulated.
32 devices in a mesh: dp: 16 (over z, y, core), tensor: 2 (over x).
Axes of the slice: x: 2, y: 2, z: 4, core: 2. Of those that a mesh axis runs over, the one named last changes fastest.
Arguments:
- block_input: bfloat16 [32768, 1024], P(('dp', 'tensor')), may hold values from -6 to 6
- mixer_gain: float32 [1024], replicated, may hold values from 0.25 to 1.75
- in_weight: bfloat16 [1024, 3, 1024], P(None, None, 'tensor'), may hold values from -0.1875 to 0.1875
- conv_kernel: bfloat16 [3, 1024], P(None, 'tensor'), may hold values from -3.5 to 3.5
- out_weight: bfloat16 [1024, 1024], P('tensor'), may hold values from -0.1875 to 0.1875
- ffn_gain: float32 [1024], replicated, may hold values from 0.25 to 1.75
- gate_weight: bfloat16 [1024, 4608], P(None, 'tensor'), may hold values from -0.1875 to 0.1875
- up_weight: bfloat16 [1024, 4608], P(None, 'tensor'), may hold values from -0.1875 to 0.1875
- down_weight: bfloat16 [4608, 1024], P('tensor'), may hold values from -0.09375 to 0.09375
- output_grad: bfloat16 [32768, 1024], P(('dp', 'tensor')), may hold values from -6 to 6
- lengths: int32 [32], P('dp'), may hold values from 256 to 1024, as said below
Outputs:
- block_output: bfloat16 [32768, 1024], P(('dp', 'tensor'))
- input_grad: bfloat16 [32768, 1024], P(('dp', 'tensor'))
- mixer_gain_grad: float32 [1024], replicated
- in_weight_grad: float32 [1024, 3, 1024], P(None, None, 'tensor')
- conv_kernel_grad: float32 [3, 1024], P(None, 'tensor')
- out_weight_grad: float32 [1024, 1024], P('tensor')
- ffn_gain_grad: float32 [1024], replicated
- gate_weight_grad: float32 [1024, 4608], P(None, 'tensor')
- up_weight_grad: float32 [1024, 4608], P(None, 'tensor')
- down_weight_grad: float32 [4608, 1024], P('tensor')
Inputs may be any that keep to these rules, and one draw needn't show every extreme that they name: `lengths`: each slot holds one sequence at positions 0 to its length - 1; some slot has length 1024 and some 1024 // 4.
All inputs are finite; a program needn't handle non-finite values.
Results may differ from a plain program's by a relative error of at most 0.022.
Values may be sent and summed in bfloat16 or wider, within the bound.
A program may use at most 256 MiB of HBM per device.

v0:
```python
import jax
import jax.numpy as jnp
from jax import lax
from jax.sharding import PartitionSpec as P

KERNEL = 3
eps = 1e-05


def rms_forward(values, gain_values):
    inverse = lax.rsqrt(jnp.mean(values * values, axis=-1, keepdims=True) + eps)
    return (values * inverse * gain_values, inverse)


def rms_backward(values, inverse, gain_values, upstream):
    weighted = upstream * gain_values
    gain_part = jnp.sum(upstream * values * inverse, axis=0)
    through = inverse * weighted - values * inverse**3 * jnp.mean(
        weighted * values, axis=-1, keepdims=True
    )
    return (through, gain_part)


def local(
    block_input,
    mixer_gain,
    in_weight,
    conv_kernel,
    out_weight,
    ffn_gain,
    gate_weight,
    up_weight,
    down_weight,
    output_grad,
    lengths,
):
    local_rows = block_input.shape[0]
    model_width = block_input.shape[1]
    channels = in_weight.shape[2]
    slot_count = lengths.shape[0]
    source = block_input.astype(jnp.float32)
    normed_one, inverse_one = rms_forward(source, mixer_gain)
    gathered_one = lax.all_gather(normed_one.astype(jnp.bfloat16), "tensor", axis=0, tiled=True)
    group_rows = gathered_one.shape[0]
    slot_length = group_rows // slot_count
    in_flat = in_weight.reshape(model_width, 3 * channels)
    projected = jnp.dot(gathered_one, in_flat, preferred_element_type=jnp.float32).reshape(
        group_rows, 3, channels
    )
    b_part = projected[:, 0]
    c_part = projected[:, 1]
    x_part = projected[:, 2]
    mixed = (b_part * x_part).reshape(slot_count, slot_length, channels)
    kernel_values = conv_kernel.astype(jnp.float32)
    padded = jnp.pad(mixed, ((0, 0), (KERNEL - 1, 0), (0, 0)))
    convolved = jnp.zeros_like(mixed)
    for offset in range(KERNEL):
        convolved = convolved + kernel_values[offset] * padded[:, offset : offset + slot_length]
    convolved = convolved.reshape(group_rows, channels)
    gated = (c_part * convolved).astype(jnp.bfloat16)
    hidden = source + lax.psum_scatter(
        jnp.dot(gated, out_weight, preferred_element_type=jnp.float32).astype(jnp.bfloat16),
        "tensor",
        scatter_dimension=0,
        tiled=True,
    ).astype(jnp.float32)
    normed_two, inverse_two = rms_forward(hidden, ffn_gain)
    gathered_two = lax.all_gather(normed_two.astype(jnp.bfloat16), "tensor", axis=0, tiled=True)
    gate_value = jnp.dot(gathered_two, gate_weight, preferred_element_type=jnp.float32)
    up_value = jnp.dot(gathered_two, up_weight, preferred_element_type=jnp.float32)
    sigmoid_gate = jax.nn.sigmoid(gate_value)
    silu_value = gate_value * sigmoid_gate
    inner_low = (silu_value * up_value).astype(jnp.bfloat16)
    block_output = (
        hidden
        + lax.psum_scatter(
            jnp.dot(inner_low, down_weight, preferred_element_type=jnp.float32).astype(
                jnp.bfloat16
            ),
            "tensor",
            scatter_dimension=0,
            tiled=True,
        ).astype(jnp.float32)
    ).astype(jnp.bfloat16)
    row_index = lax.axis_index("tensor") * local_rows + jnp.arange(local_rows, dtype=jnp.int32)
    slot_of = row_index // slot_length
    position = row_index % slot_length
    matched = (slot_of[:, None] == jnp.arange(slot_count, dtype=jnp.int32)[None, :]) & (
        position[:, None] < lengths[None, :]
    )
    token_mask = jnp.any(matched, axis=1).astype(jnp.float32)
    cotangent = output_grad.astype(jnp.float32) * token_mask[:, None]
    grad_rows = lax.all_gather(cotangent.astype(jnp.bfloat16), "tensor", axis=0, tiled=True)
    inner_grad = jnp.einsum("rd,fd->rf", grad_rows, down_weight, preferred_element_type=jnp.float32)
    down_weight_grad = jnp.einsum(
        "rf,rd->fd", inner_low, grad_rows, preferred_element_type=jnp.float32
    )
    gate_grad = (
        inner_grad * up_value * sigmoid_gate * (1.0 + gate_value * (1.0 - sigmoid_gate))
    ).astype(jnp.bfloat16)
    up_grad = (inner_grad * silu_value).astype(jnp.bfloat16)
    gate_weight_grad = jnp.einsum(
        "rd,rf->df", gathered_two, gate_grad, preferred_element_type=jnp.float32
    )
    up_weight_grad = jnp.einsum(
        "rd,rf->df", gathered_two, up_grad, preferred_element_type=jnp.float32
    )
    from_gate = jnp.einsum("rf,df->rd", gate_grad, gate_weight, preferred_element_type=jnp.float32)
    normed_two_grad = lax.psum_scatter(
        (
            from_gate
            + jnp.einsum("rf,df->rd", up_grad, up_weight, preferred_element_type=jnp.float32)
        ).astype(jnp.bfloat16),
        "tensor",
        scatter_dimension=0,
        tiled=True,
    ).astype(jnp.float32)
    through_two, ffn_gain_part = rms_backward(hidden, inverse_two, ffn_gain, normed_two_grad)
    hidden_grad = cotangent + through_two
    hidden_rows = lax.all_gather(hidden_grad.astype(jnp.bfloat16), "tensor", axis=0, tiled=True)
    gated_grad = jnp.einsum(
        "rd,cd->rc", hidden_rows, out_weight, preferred_element_type=jnp.float32
    )
    out_weight_grad = jnp.einsum(
        "rc,rd->cd", gated, hidden_rows, preferred_element_type=jnp.float32
    )
    c_grad = gated_grad * convolved
    conv_grad = (gated_grad * c_part).reshape(slot_count, slot_length, channels)
    padded_after = jnp.pad(conv_grad, ((0, 0), (0, KERNEL - 1), (0, 0)))
    mixed_grad = jnp.zeros_like(conv_grad)
    kernel_rows = []
    for offset in range(KERNEL):
        shift_start = KERNEL - 1 - offset
        mixed_grad = (
            mixed_grad
            + kernel_values[offset] * padded_after[:, shift_start : shift_start + slot_length]
        )
        kernel_rows.append(
            jnp.sum(conv_grad * padded[:, offset : offset + slot_length], axis=(0, 1))
        )
    conv_kernel_grad = jnp.stack(kernel_rows, axis=0)
    mixed_grad = mixed_grad.reshape(group_rows, channels)
    projected_grad = jnp.stack([mixed_grad * x_part, c_grad, mixed_grad * b_part], axis=1).astype(
        jnp.bfloat16
    )
    in_weight_grad = jnp.einsum(
        "rd,rkc->dkc", gathered_one, projected_grad, preferred_element_type=jnp.float32
    )
    normed_one_grad = lax.psum_scatter(
        jnp.einsum(
            "rkc,dkc->rd", projected_grad, in_weight, preferred_element_type=jnp.float32
        ).astype(jnp.bfloat16),
        "tensor",
        scatter_dimension=0,
        tiled=True,
    ).astype(jnp.float32)
    through_one, mixer_gain_part = rms_backward(source, inverse_one, mixer_gain, normed_one_grad)
    input_grad = (hidden_grad + through_one).astype(jnp.bfloat16)
    (
        in_weight_grad,
        conv_kernel_grad,
        out_weight_grad,
        gate_weight_grad,
        up_weight_grad,
        down_weight_grad,
    ) = (
        lax.psum(in_weight_grad.astype(jnp.bfloat16), "dp").astype(jnp.float32),
        lax.psum(conv_kernel_grad.astype(jnp.bfloat16), "dp").astype(jnp.float32),
        lax.psum(out_weight_grad.astype(jnp.bfloat16), "dp").astype(jnp.float32),
        lax.psum(gate_weight_grad.astype(jnp.bfloat16), "dp").astype(jnp.float32),
        lax.psum(up_weight_grad.astype(jnp.bfloat16), "dp").astype(jnp.float32),
        lax.psum(down_weight_grad.astype(jnp.bfloat16), "dp").astype(jnp.float32),
    )
    mixer_gain_grad, ffn_gain_grad = lax.psum((mixer_gain_part, ffn_gain_part), ("dp", "tensor"))
    return (
        block_output,
        input_grad,
        mixer_gain_grad,
        in_weight_grad,
        conv_kernel_grad,
        out_weight_grad,
        ffn_gain_grad,
        gate_weight_grad,
        up_weight_grad,
        down_weight_grad,
    )


def solution(mesh):
    return jax.shard_map(
        local,
        mesh=mesh,
        in_specs=(
            P(("dp", "tensor"), None),
            P(),
            P(None, None, "tensor"),
            P(None, "tensor"),
            P("tensor", None),
            P(),
            P(None, "tensor"),
            P(None, "tensor"),
            P("tensor", None),
            P(("dp", "tensor"), None),
            P("dp"),
        ),
        out_specs=(
            P(("dp", "tensor"), None),
            P(("dp", "tensor"), None),
            P(),
            P(None, None, "tensor"),
            P(None, "tensor"),
            P("tensor", None),
            P(),
            P(None, "tensor"),
            P(None, "tensor"),
            P("tensor", None),
        ),
        check_vma=False,
    )
```

profile of v0, /device:TPU:0, one launch (start us, length us, event | category | flops | bytes accessed | tf_op | source)
XLA Modules:
  0.0 967.7 jit_solution(12564560113143871038)
XLA Ops:
  18.8 54.9 %all-gather.5.cloned.1.call-done = bf16[2048,1024]{1,0:T(8,128)(2,1)} async-done(((bf16[1024,1024]{1,0:T(8,128)(2,1)}), bf16[2048,1024]{1,0:T(8,128)(2,1)}) %all-gather.5.cloned.1.call-update) | async-done | bytes 4194320 | tf_op jit(solution)/shard_map/all_gather | solution.py:43
  73.7 9.4 fusion.26
  96.6 54.4 %reduce-scatter.5.cloned.1.call-done = bf16[1024,1024]{1,0:T(8,128)(2,1)} async-done(((bf16[2048,1024]{1,0:T(8,128)(2,1)}), bf16[1024,1024]{1,0:T(8,128)(2,1)}) %reduce-scatter.5.cloned.1.call-update) | async-done | bytes 2097168 | tf_op jit(solution)/shard_map/reduce_scatter | solution.py:61
  161.5 52.2 %all-gather.7.cloned.1.call-done = bf16[2048,1024]{1,0:T(8,128)(2,1)} async-done(((bf16[1024,1024]{1,0:T(8,128)(2,1)}), bf16[2048,1024]{1,0:T(8,128)(2,1)}) %all-gather.7.cloned.1.call-update) | async-done | bytes 4194320 | tf_op jit(solution)/shard_map/all_gather | solution.py:68
  213.7 16.9 %fusion.46 = f32[2048,2304]{1,0:T(8,128)} fusion(bf16[2048,1024]{1,0:T(8,128)(2,1)} %all-gather.7.cloned.1.call-done, bf16[1024,2304]{1,0:T(8,128)(2,1)} %param.18), kind=kOutput, calls=%fused_computation.96 | convolution fusion | flops 9663676416 | bytes 27787264 | tf_op jit(solution)/shard_map/dot_general | solution.py:70
  230.6 15.3 %fusion.45 = f32[2048,2304]{1,0:T(8,128)} fusion(bf16[2048,1024]{1,0:T(8,128)(2,1)S(1)} %copy-done.37, bf16[1024,2304]{1,0:T(8,128)(2,1)} %param.17), kind=kOutput, calls=%fused_computation.95 | convolution fusion | flops 9663676416 | bytes 27787264 | tf_op jit(solution)/shard_map/dot_general | solution.py:69
  245.9 26.7 %all-gather.9.cloned.1.call-done = bf16[2048,1024]{1,0:T(8,128)(2,1)} async-done(((bf16[1024,1024]{1,0:T(8,128)(2,1)}), bf16[2048,1024]{1,0:T(8,128)(2,1)}) %all-gather.9.cloned.1.call-update) | async-done | bytes 4194320 | tf_op jit(solution)/shard_map/all_gather | solution.py:93
  272.6 35.7 %multiply_convert_fusion = (bf16[2048,2304]{1,0:T(8,128)(2,1)}, bf16[2048,2304]{1,0:T(8,128)(2,1)}, bf16[2048,2304]{1,0:T(8,128)(2,1)}) fusion(f32[2048,2304]{1,0:T(8,128)} %fusion.45, f32[2048,2304]{1,0:T(8,128)} %fusion.46, bf16[2048,1024]{1,0:T(8,128)(2,1)} %all-gather.9.cloned.1.call-done, bf16[2304,1024]{1,0:T(8,128)(2,1)} %param.19), kind=kOutput, calls=%fused_computation | convolution fusion | flops 9734455296 | bytes 74973184 | tf_op jit(solution)/shard_map/rd,fd->rf/dot_general | solution.py:94
  308.2 14.0 %fusion.47 = f32[2048,1024]{1,0:T(8,128)S(1)} fusion(bf16[2048,2304]{1,0:T(8,128)(2,1)} %get-tuple-element.27, bf16[1024,2304]{1,0:T(8,128)(2,1)} %param.17), kind=kOutput, calls=%fused_computation.97 | convolution fusion | flops 9663676416 | bytes 22544384 | tf_op jit(solution)/shard_map/rf,df->rd/dot_general | solution.py:108
  322.3 14.3 %add_convert_fusion = bf16[2048,1024]{1,0:T(8,128)(2,1)} fusion(f32[2048,1024]{1,0:T(8,128)S(1)} %fusion.47, bf16[2048,2304]{1,0:T(8,128)(2,1)S(1)} %copy-done.39, bf16[1024,2304]{1,0:T(8,128)(2,1)} %param.18), kind=kOutput, calls=%fused_computation.12 | convolution fusion | flops 9667870720 | bytes 26738688 | tf_op jit(solution)/shard_map/rf,df->rd/dot_general | solution.py:112
  336.7 15.2 %convolution_convert_fusion.3 = bf16[2048,1024]{1,0:T(8,128)(2,1)} fusion(bf16[2048,2304]{1,0:T(8,128)(2,1)} %get-tuple-element.28, bf16[2304,1024]{1,0:T(8,128)(2,1)} %param.19), kind=kOutput, calls=%fused_computation.66 | convolution fusion | flops 9665773568 | bytes 18350080 | tf_op jit(solution)/shard_map/dot_general | solution.py:77
  352.0 39.1 %reduce-scatter.9.cloned.1.call-done = bf16[1024,1024]{1,0:T(8,128)(2,1)} async-done(((bf16[2048,1024]{1,0:T(8,128)(2,1)}), bf16[1024,1024]{1,0:T(8,128)(2,1)}) %reduce-scatter.9.cloned.1.call-update) | async-done | bytes 2097168 | tf_op jit(solution)/shard_map/reduce_scatter | solution.py:109
  395.0 52.6 %reduce-scatter.7.cloned.1.call-done = bf16[1024,1024]{1,0:T(8,128)(2,1)} async-done(((bf16[2048,1024]{1,0:T(8,128)(2,1)}), bf16[1024,1024]{1,0:T(8,128)(2,1)}) %reduce-scatter.7.cloned.1.call-update) | async-done | bytes 2097168 | tf_op jit(solution)/shard_map/reduce_scatter | solution.py:76
  454.4 56.8 %all-gather.11.cloned.1.call-done = bf16[2048,1024]{1,0:T(8,128)(2,1)} async-done(((bf16[1024,1024]{1,0:T(8,128)(2,1)}), bf16[2048,1024]{1,0:T(8,128)(2,1)}) %all-gather.11.cloned.1.call-update) | async-done | bytes 4194320 | tf_op jit(solution)/shard_map/all_gather | solution.py:120
  511.3 10.4 %multiply_reduce_fusion.1 = (bf16[512]{0:T(512)(128)(2,1)S(1)}, bf16[512]{0:T(512)(128)(2,1)S(1)}, f32[2048,512]{1,0:T(8,128)}, f32[2048,512]{1,0:T(8,128)}) fusion(f32[2,1024,512]{2,1,0:T(8,128)} %bitcast.78, f32[2048,3,512]{2,0,1:T(8,128)} %copy-done.3, bf16[2048,1024]{1,0:T(8,128)(2,1)} %all-gather.11.cloned.1.call-done, bf16[512,1024]{1,0:T(8,128)(2,1)S(1)} %copy-done), kind=kOutput, calls=%fused_computation.54 | convolution fusion | flops 2152725504 | bytes 22022144 | tf_op jit(solution)/shard_map/rd,cd->rc/dot_general | solution.py:121
  526.8 8.4 multiply_add_fusion
  541.3 10.1 %bitcast_convert_fusion = bf16[2048,1024]{1,0:T(8,128)(2,1)} fusion(bf16[1024,3,512]{2,0,1:T(8,128)(2,1)S(1)} %copy-done.10, bf16[2048,1,512]{2,0,1:T(8,128)(2,1)} %get-tuple-element.30, bf16[2048,1,512]{2,0,1:T(8,128)(2,1)} %bitcast.84, bf16[2048,1,512]{2,0,1:T(8,128)(2,1)} %get-tuple-element.29), kind=kOutput, calls=%fused_computation.11 | convolution fusion | flops 6450839552 | bytes 13631488 | tf_op jit(solution)/shard_map/rkc,dkc->rd/dot_general | solution.py:150
  551.5 15.6 %convolution_convert_fusion.2 = bf16[2304,1024]{1,0:T(8,128)(2,1)} fusion(bf16[2048,2304]{1,0:T(8,128)(2,1)} %get-tuple-element.28, bf16[2048,1024]{1,0:T(8,128)(2,1)} %all-gather.9.cloned.1.call-done), kind=kOutput, calls=%fused_computation.16 | convolution fusion | flops 9666035712 | bytes 18350080 | tf_op jit(solution)/shard_map/rf,rd->fd/dot_general | solution.py:95
  567.1 14.1 %convolution_convert_fusion = bf16[1024,2304]{1,0:T(8,128)(2,1)} fusion(bf16[2048,1024]{1,0:T(8,128)(2,1)S(1)} %copy-done.38, bf16[2048,2304]{1,0:T(8,128)(2,1)} %get-tuple-element.26), kind=kOutput, calls=%fused_computation.14 | convolution fusion | flops 9666035712 | bytes 18350080 | tf_op jit(solution)/shard_map/rd,rf->df/dot_general | solution.py:105
  581.2 12.3 %convolution_convert_fusion.1 = bf16[1024,2304]{1,0:T(8,128)(2,1)} fusion(bf16[2048,1024]{1,0:T(8,128)(2,1)S(1)} %copy-done.38, bf16[2048,2304]{1,0:T(8,128)(2,1)S(1)} %bitcast.93), kind=kOutput, calls=%fused_computation.15 | convolution fusion | flops 9666035712 | bytes 18350080 | tf_op jit(solution)/shard_map/rd,rf->df/dot_general | solution.py:102
  598.2 8.5 fusion.31
  612.2 34.8 %psum.58 = bf16[3,512]{1,0:T(4,128)(2,1)S(1)} all-reduce(bf16[3,512]{1,0:T(4,128)(2,1)S(1)} %pad_maximum_fusion.5), channel_id=1, replica_groups=mesh['dp'=16,'tensor'=2] {'dp'}, use_global_device_ids=true, to_apply=%region_15.16 | all-reduce | flops 1536 | bytes 6144 | tf_op jit(solution)/shard_map/psum | solution.py:168
  650.9 38.5 %all-reduce.2 = (f32[1024]{0:T(1024)}, f32[1024]{0:T(1024)}) all-reduce(f32[1024]{0:T(1024)S(1)} %get-tuple-element.14, f32[1024]{0:T(1024)S(1)} %get-tuple-element.12), channel_id=1, replica_groups=mesh['dp'=16,'tensor'=2] {'dp','tensor'}, use_global_device_ids=true, to_apply=%region_10.11 | all-reduce | flops 2048 | bytes 16384 | tf_op jit(solution)/shard_map/psum | solution.py:174
  694.0 245.0 %all-reduce.6.cloned.1.call-done = (bf16[1024,3,512]{2,0,1:T(8,128)(2,1)}, bf16[512,1024]{1,0:T(8,128)(2,1)}, bf16[1024,2304]{1,0:T(8,128)(2,1)}, bf16[1024,2304]{1,0:T(8,128)(2,1)}, bf16[2304,1024]{1,0:T(8,128)(2,1)}) async-done(((bf16[1024,3,512]{2,0,1:T(8,128)(2,1)}, bf16[512,1024]{1,0:T(8,128)(2,1)}, bf16[1024,2304]{1,0:T(8,128)(2,1)}, bf16[1024,2304]{1,0:T(8,128)(2,1)}, bf16[2304,1024]{1,0:T(8,128)(2,1)}), ...) | async-done | bytes 18350096 | tf_op jit(solution)/shard_map/psum | solution.py:167
  (159 shorter events, 98.0 us)
Async XLA Ops:
  7.2 85.0 %copy-start = (bf16[512,1024]{1,0:T(8,128)(2,1)S(1)}, bf16[512,1024]{1,0:T(8,128)(2,1)}, u32[]{:S(2)}) copy-start(bf16[512,1024]{1,0:T(8,128)(2,1)} %param.15) | copy-start | bytes 3145732
  7.2 66.5 %all-gather.5.cloned.1.call-start = ((), (), s32[]{:S(2)}) async-start(), calls=%async_computation.4 | async-start | bytes 6291456 | tf_op jit(solution)/shard_map/all_gather | solution.py:43
  14.1 137.0 %reduce-scatter.5.cloned.1.call-start = ((), (), s32[]{:S(2)}) async-start(), calls=%async_computation.5 | async-start | bytes 6291456 | tf_op jit(solution)/shard_map/reduce_scatter | solution.py:61
  18.8 65.4 %copy-start.26 = (f32[1,512]{1,0:T(1,128)}, f32[1,512]{1,0:T(1,128)S(1)}, u32[]{:S(2)}) copy-start(f32[1,512]{1,0:T(1,128)S(1)} %get-tuple-element.36) | copy-start | bytes 6148
  18.8 65.4 %copy-start.28 = (f32[1,512]{1,0:T(1,128)}, f32[1,512]{1,0:T(1,128)S(1)}, u32[]{:S(2)}) copy-start(f32[1,512]{1,0:T(1,128)S(1)} %get-tuple-element.37) | copy-start | bytes 6148
  18.8 65.4 %copy-start.30 = (f32[1,512]{1,0:T(1,128)}, f32[1,512]{1,0:T(1,128)S(1)}, u32[]{:S(2)}) copy-start(f32[1,512]{1,0:T(1,128)S(1)} %get-tuple-element.38) | copy-start | bytes 6148
  96.5 54.5 %copy-start.1 = (bf16[1024,1024]{1,0:T(8,128)(2,1)S(1)}, bf16[1024,1024]{1,0:T(8,128)(2,1)}, u32[]{:S(2)}) copy-start(bf16[1024,1024]{1,0:T(8,128)(2,1)} %param.11) | copy-start | bytes 6291460
  96.5 58.2 %copy-start.21 = (f32[1024]{0:T(1024)S(1)}, f32[1024]{0:T(1024)}, u32[]{:S(2)}) copy-start(f32[1024]{0:T(1024)} %param.16) | copy-start | bytes 12292
  96.6 117.2 %all-gather.7.cloned.1.call-start = ((), (), s32[]{:S(2)}) async-start(), calls=%async_computation.6 | async-start | bytes 6291456 | tf_op jit(solution)/shard_map/all_gather | solution.py:68
  156.8 115.7 %all-gather.9.cloned.1.call-start = ((), (), s32[]{:S(2)}) async-start(), calls=%async_computation.8 | async-start | bytes 6291456 | tf_op jit(solution)/shard_map/all_gather | solution.py:93
  161.5 229.6 %reduce-scatter.9.cloned.1.call-start = ((), (), s32[]{:S(2)}) async-start(), calls=%async_computation.9 | async-start | bytes 6291456 | tf_op jit(solution)/shard_map/reduce_scatter | solution.py:109
  336.6 111.0 %reduce-scatter.7.cloned.1.call-start = ((), (), s32[]{:S(2)}) async-start(), calls=%async_computation.7 | async-start | bytes 6291456 | tf_op jit(solution)/shard_map/reduce_scatter | solution.py:76
  351.9 39.2 %copy-start.2 = (bf16[1024,1024]{1,0:T(8,128)(2,1)S(1)}, bf16[1024,1024]{1,0:T(8,128)(2,1)}, u32[]{:S(2)}) copy-start(bf16[1024,1024]{1,0:T(8,128)(2,1)} %param.11) | copy-start | bytes 6291460
  351.9 39.2 %copy-start.20 = (f32[1024]{0:T(1024)S(1)}, f32[1024]{0:T(1024)}, u32[]{:S(2)}) copy-start(f32[1024]{0:T(1024)} %copy-done.19) | copy-start | bytes 12292
  351.9 39.2 %copy-start.22 = (f32[1024]{0:T(1024)S(1)}, f32[1024]{0:T(1024)}, u32[]{:S(2)}) copy-start(f32[1024]{0:T(1024)} %param.16) | copy-start | bytes 12292
  351.9 95.7 %copy-start.25 = (f32[1024]{0:T(1024)S(1)}, f32[1024]{0:T(1024)}, u32[]{:S(2)}) copy-start(f32[1024]{0:T(1024)} %copy-done.24) | copy-start | bytes 12292
  351.9 95.7 %copy-start.33 = (f32[1024]{0:T(1024)S(1)}, f32[1024]{0:T(1024)}, u32[]{:S(2)}) copy-start(f32[1024]{0:T(1024)} %get-tuple-element.34) | copy-start | bytes 12292
  351.9 159.4 %all-gather.11.cloned.1.call-start = ((), (), s32[]{:S(2)}) async-start(), calls=%async_computation.10 | async-start | bytes 6291456 | tf_op jit(solution)/shard_map/all_gather | solution.py:120
  454.4 193.3 %reduce-scatter.11.cloned.1.call-start = ((), (), s32[]{:S(2)}) async-start(), calls=%async_computation.11 | async-start | bytes 6291456 | tf_op jit(solution)/shard_map/reduce_scatter | solution.py:149
  551.4 387.6 %all-reduce.6.cloned.1.call-start = ((), (), s32[]{:S(2)}) async-start(), calls=%async_computation.12 | async-start | bytes 36700160 | tf_op jit(solution)/shard_map/psum | solution.py:167
  551.5 29.7 %slice-start.7 = ((s8[9437184]{0:T(1024)(128)(4,1)}), s8[4194304]{0:T(1024)(128)(4,1)S(1)}, s32[]{:S(2)}) async-start(s8[9437184]{0:T(1024)(128)(4,1)} %bitcast.92), calls=%async_computation.20 | async-start | bytes 8388608
  606.7 41.0 %copy-start.18 = (f32[1024]{0:T(1024)S(1)}, f32[1024]{0:T(1024)}, u32[]{:S(2)}) copy-start(f32[1024]{0:T(1024)} %copy-done.17) | copy-start | bytes 12292
  606.7 41.0 %copy-start.23 = (f32[1024]{0:T(1024)S(1)}, f32[1024]{0:T(1024)}, u32[]{:S(2)}) copy-start(f32[1024]{0:T(1024)} %param.12) | copy-start | bytes 12292
  612.2 77.3 %copy-start.32 = (f32[1024]{0:T(1024)S(1)}, f32[1024]{0:T(1024)}, u32[]{:S(2)}) copy-start(f32[1024]{0:T(1024)} %get-tuple-element.32) | copy-start | bytes 12292
  (35 other events, 284.8 us)
Sparse Core Ops, SparseCore 0:
  14.2 59.4 all-gather.4
  96.7 54.2 reduce-scatter.4
  156.9 56.7 all-gather.6
  215.8 56.7 all-gather.8
  336.7 54.3 reduce-scatter.8
  393.2 54.3 reduce-scatter.6
  454.5 56.7 all-gather.10
  551.5 54.3 reduce-scatter.10
  612.1 326.8 all-reduce.5
where the time goes:
time: 976 us; the launch traced here: 968 us
  waiting for transfers between devices  582 us (60%)
  matrix products  200 us (20%)
  other arithmetic  84.3 us (9%)
  blocking collectives  73.3 us (8%)
  between operations  14.6 us (1%)
  local copies, waits for them, and re-layouts  13.3 us (1%)
    psum x1, waiting for transfers between devices, local(): lax.psum(in_weight_grad.astype(jnp.bfloat16), 'dp').astype(jnp.float32)  245 us
    all_gather x1, waiting for transfers between devices, local(): lax.all_gather(hidden_grad.astype(jnp.bfloat16), 'tensor', axis=0, tiled=...  56.8 us
    all_gather x1, waiting for transfers between devices, local(): lax.all_gather(normed_one.astype(jnp.bfloat16), 'tensor', axis=0, tiled=T...  54.9 us
    reduce_scatter x1, waiting for transfers between devices, local(): lax.psum_scatter(jnp.dot(gated, out_weight, preferred_element_type=jnp.fl...  54.4 us
    reduce_scatter x1, waiting for transfers between devices, local(): lax.psum_scatter(jnp.dot(inner_low, down_weight, preferred_element_type=j...  52.6 us
    all_gather x1, waiting for transfers between devices, local(): lax.all_gather(normed_two.astype(jnp.bfloat16), 'tensor', axis=0, tiled=T...  52.2 us
    reduce_scatter x1, waiting for transfers between devices, local(): lax.psum_scatter((from_gate + jnp.einsum('rf,df->rd', up_grad, up_weight,...  39.1 us
    psum x1, blocking collectives, local(): lax.psum((mixer_gain_part, ffn_gain_part), ('dp', 'tensor'))  38.5 us
  transfers between devices with their start and end apart: 9, of which 8 were waited for; matrix products, arithmetic and copies ran while one was open for 13% of the time, Pallas kernels for 0%

commit v1 on v0

--- a/solution.py
+++ b/solution.py
@@ -164,7 +164,9 @@
         up_weight_grad,
         down_weight_grad,
     ) = (
-        lax.psum(in_weight_grad.astype(jnp.bfloat16), "dp").astype(jnp.float32),
+        jnp.sum(lax.all_gather(in_weight_grad.astype(jnp.bfloat16), "dp"), axis=0).astype(
+            jnp.float32
+        ),
         lax.psum(conv_kernel_grad.astype(jnp.bfloat16), "dp").astype(jnp.float32),
         lax.psum(out_weight_grad.astype(jnp.bfloat16), "dp").astype(jnp.float32),
         lax.psum(gate_weight_grad.astype(jnp.bfloat16), "dp").astype(jnp.float32),

time: 976 us -> 1150 us (1.18)
  waiting for transfers between devices: 582 us -> 714 us
  other arithmetic: 84.3 us -> 118 us
    all_gather x0 -> x1, waiting for transfers between devices: none -> 201 us  [local(): lax.all_gather(in_weight_grad.astype(jnp.bfloat16), 'dp')]
    psum x1, waiting for transfers between devices: 245 us -> 181 us  [local(): lax.psum(out_weight_grad.astype(jnp.bfloat16), 'dp').astype(jnp.float32)]
    all_gather x1, waiting for transfers between devices: 56.8 us -> 14.8 us  [local(): lax.all_gather(hidden_grad.astype(jnp.bfloat16), 'tensor', axis=0, tiled=...]
    reduce_scatter x1, waiting for transfers between devices: 0.01 us -> 37.1 us  [local(): lax.psum_scatter(jnp.einsum('rkc,dkc->rd', projected_grad, in_weight, pre...]
    reduce_sum x0 -> x1, other arithmetic: none -> 18.3 us  [local(): jnp.sum(lax.all_gather(in_weight_grad.astype(jnp.bfloat16), 'dp'), axis=0)]
  transfers between devices with their start and end apart: 9 -> 10, of which waited for: 8 -> 10; matrix products, arithmetic and copies ran while one was open for 13% -> 17% of each run, Pallas kernels for 0% -> 0%
where the time goes in v1:
time: 1150 us; the launch traced here: 1140 us
  waiting for transfers between devices  714 us (62%)
  matrix products  209 us (18%)
  other arithmetic  118 us (10%)
  blocking collectives  75.5 us (7%)
  between operations  15 us (1%)
    all_gather x1, waiting for transfers between devices, local(): lax.all_gather(in_weight_grad.astype(jnp.bfloat16), 'dp')  201 us
    psum x1, waiting for transfers between devices, local(): lax.psum(out_weight_grad.astype(jnp.bfloat16), 'dp').astype(jnp.float32)  181 us
    all_gather x1, waiting for transfers between devices, local(): lax.all_gather(normed_one.astype(jnp.bfloat16), 'tensor', axis=0, tiled=T...  54.9 us
    reduce_scatter x1, waiting for transfers between devices, local(): lax.psum_scatter(jnp.dot(gated, out_weight, preferred_element_type=jnp.fl...  54.2 us
    all_gather x1, waiting for transfers between devices, local(): lax.all_gather(normed_two.astype(jnp.bfloat16), 'tensor', axis=0, tiled=T...  53.3 us
    reduce_scatter x1, waiting for transfers between devices, local(): lax.psum_scatter(jnp.dot(inner_low, down_weight, preferred_element_type=j...  52.5 us
    psum x1, blocking collectives, local(): lax.psum((mixer_gain_part, ffn_gain_part), ('dp', 'tensor'))  40.7 us
    reduce_scatter x1, waiting for transfers between devices, local(): lax.psum_scatter((from_gate + jnp.einsum('rf,df->rd', up_grad, up_weight,...  38.7 us
  transfers between devices with their start and end apart: 10, of which 10 were waited for; matrix products, arithmetic and copies ran while one was open for 17% of the time, Pallas kernels for 0%

profile of v1, /device:TPU:0, one launch (start us, length us, event | category | flops | bytes accessed | tf_op | source)
XLA Modules:
  0.0 1139.1 jit_solution(5501214581542693112)
XLA Ops:
  18.2 54.9 %all-gather.7.cloned.1.call-done = bf16[2048,1024]{1,0:T(8,128)(2,1)} async-done(((bf16[1024,1024]{1,0:T(8,128)(2,1)}), bf16[2048,1024]{1,0:T(8,128)(2,1)}) %all-gather.7.cloned.1.call-update) | async-done | bytes 4194320 | tf_op jit(solution)/shard_map/all_gather | solution.py:43
  102.4 54.2 %reduce-scatter.5.cloned.1.call-done = bf16[1024,1024]{1,0:T(8,128)(2,1)} async-done(((bf16[2048,1024]{1,0:T(8,128)(2,1)}), bf16[1024,1024]{1,0:T(8,128)(2,1)}) %reduce-scatter.5.cloned.1.call-update) | async-done | bytes 2097168 | tf_op jit(solution)/shard_map/reduce_scatter | solution.py:61
  166.0 53.3 %all-gather.9.cloned.1.call-done = bf16[2048,1024]{1,0:T(8,128)(2,1)} async-done(((bf16[1024,1024]{1,0:T(8,128)(2,1)}), bf16[2048,1024]{1,0:T(8,128)(2,1)}) %all-gather.9.cloned.1.call-update) | async-done | bytes 4194320 | tf_op jit(solution)/shard_map/all_gather | solution.py:68
  219.3 16.9 %fusion.46 = f32[2048,2304]{1,0:T(8,128)} fusion(bf16[2048,1024]{1,0:T(8,128)(2,1)} %all-gather.9.cloned.1.call-done, bf16[1024,2304]{1,0:T(8,128)(2,1)} %param.18), kind=kOutput, calls=%fused_computation.96 | convolution fusion | flops 9663676416 | bytes 27787264 | tf_op jit(solution)/shard_map/dot_general | solution.py:70
  236.1 15.3 %fusion.45 = f32[2048,2304]{1,0:T(8,128)} fusion(bf16[2048,1024]{1,0:T(8,128)(2,1)S(1)} %copy-done.27, bf16[1024,2304]{1,0:T(8,128)(2,1)} %param.17), kind=kOutput, calls=%fused_computation.95 | convolution fusion | flops 9663676416 | bytes 27787264 | tf_op jit(solution)/shard_map/dot_general | solution.py:69
  251.4 26.7 %all-gather.11.cloned.1.call-done = bf16[2048,1024]{1,0:T(8,128)(2,1)} async-done(((bf16[1024,1024]{1,0:T(8,128)(2,1)}), bf16[2048,1024]{1,0:T(8,128)(2,1)}) %all-gather.11.cloned.1.call-update) | async-done | bytes 4194320 | tf_op jit(solution)/shard_map/all_gather | solution.py:93
  278.1 35.6 %multiply_convert_fusion = (bf16[2048,2304]{1,0:T(8,128)(2,1)}, bf16[2048,2304]{1,0:T(8,128)(2,1)}, bf16[2048,2304]{1,0:T(8,128)(2,1)}) fusion(f32[2048,2304]{1,0:T(8,128)} %fusion.45, f32[2048,2304]{1,0:T(8,128)} %fusion.46, bf16[2048,1024]{1,0:T(8,128)(2,1)} %all-gather.11.cloned.1.call-done, bf16[2304,1024]{1,0:T(8,128)(2,1)} %param.19), kind=kOutput, calls=%fused_computation | convolution fusion | flops 9734455296 | bytes 74973184 | tf_op jit(solution)/shard_map/rd,fd->rf/dot_general | solution.py:94
  313.7 16.1 %fusion.47 = f32[2048,1024]{1,0:T(8,128)} fusion(bf16[2048,2304]{1,0:T(8,128)(2,1)} %get-tuple-element.26, bf16[1024,2304]{1,0:T(8,128)(2,1)} %param.17), kind=kOutput, calls=%fused_computation.97 | convolution fusion | flops 9663676416 | bytes 22544384 | tf_op jit(solution)/shard_map/rf,df->rd/dot_general | solution.py:108
  329.8 14.6 %add_convert_fusion = bf16[2048,1024]{1,0:T(8,128)(2,1)} fusion(f32[2048,1024]{1,0:T(8,128)} %fusion.47, bf16[2048,2304]{1,0:T(8,128)(2,1)S(1)} %copy-done.29, bf16[1024,2304]{1,0:T(8,128)(2,1)} %param.18), kind=kOutput, calls=%fused_computation.12 | convolution fusion | flops 9667870720 | bytes 26738688 | tf_op jit(solution)/shard_map/rf,df->rd/dot_general | solution.py:112
  344.4 15.7 %convolution_convert_fusion.3 = bf16[2048,1024]{1,0:T(8,128)(2,1)} fusion(bf16[2048,2304]{1,0:T(8,128)(2,1)} %get-tuple-element.27, bf16[2304,1024]{1,0:T(8,128)(2,1)} %param.19), kind=kOutput, calls=%fused_computation.66 | convolution fusion | flops 9665773568 | bytes 18350080 | tf_op jit(solution)/shard_map/dot_general | solution.py:77
  360.2 38.7 %reduce-scatter.9.cloned.1.call-done = bf16[1024,1024]{1,0:T(8,128)(2,1)} async-done(((bf16[2048,1024]{1,0:T(8,128)(2,1)}), bf16[1024,1024]{1,0:T(8,128)(2,1)}) %reduce-scatter.9.cloned.1.call-update) | async-done | bytes 2097168 | tf_op jit(solution)/shard_map/reduce_scatter | solution.py:109
  402.8 52.5 %reduce-scatter.7.cloned.1.call-done = bf16[1024,1024]{1,0:T(8,128)(2,1)} async-done(((bf16[2048,1024]{1,0:T(8,128)(2,1)}), bf16[1024,1024]{1,0:T(8,128)(2,1)}) %reduce-scatter.7.cloned.1.call-update) | async-done | bytes 2097168 | tf_op jit(solution)/shard_map/reduce_scatter | solution.py:76
  462.2 15.6 %convolution_convert_fusion.2 = bf16[2304,1024]{1,0:T(8,128)(2,1)} fusion(bf16[2048,2304]{1,0:T(8,128)(2,1)} %get-tuple-element.27, bf16[2048,1024]{1,0:T(8,128)(2,1)} %all-gather.11.cloned.1.call-done), kind=kOutput, calls=%fused_computation.16 | convolution fusion | flops 9666035712 | bytes 18350080 | tf_op jit(solution)/shard_map/rf,rd->fd/dot_general | solution.py:95
  477.8 14.1 %convolution_convert_fusion = bf16[1024,2304]{1,0:T(8,128)(2,1)} fusion(bf16[2048,1024]{1,0:T(8,128)(2,1)S(1)} %copy-done.28, bf16[2048,2304]{1,0:T(8,128)(2,1)} %get-tuple-element.25), kind=kOutput, calls=%fused_computation.14 | convolution fusion | flops 9666035712 | bytes 18350080 | tf_op jit(solution)/shard_map/rd,rf->df/dot_general | solution.py:105
  491.9 12.3 %convolution_convert_fusion.1 = bf16[1024,2304]{1,0:T(8,128)(2,1)} fusion(bf16[2048,1024]{1,0:T(8,128)(2,1)S(1)} %copy-done.28, bf16[2048,2304]{1,0:T(8,128)(2,1)S(1)} %bitcast.95), kind=kOutput, calls=%fused_computation.15 | convolution fusion | flops 9666035712 | bytes 18350080 | tf_op jit(solution)/shard_map/rd,rf->df/dot_general | solution.py:102
  504.2 14.8 %all-gather.13.cloned.1.call-done = bf16[2048,1024]{1,0:T(8,128)(2,1)} async-done(((bf16[1024,1024]{1,0:T(8,128)(2,1)}), bf16[2048,1024]{1,0:T(8,128)(2,1)}) %all-gather.13.cloned.1.call-update) | async-done | bytes 4194320 | tf_op jit(solution)/shard_map/all_gather | solution.py:120
  525.4 10.3 multiply_reduce_fusion.1
  567.1 12.1 %fusion.31 = bf16[1024,3,512]{2,0,1:T(8,128)(2,1)} fusion(bf16[2048,1,512]{2,0,1:T(8,128)(2,1)} %get-tuple-element.29, bf16[2048,1,512]{2,0,1:T(8,128)(2,1)} %bitcast.87, bf16[2048,1,512]{2,0,1:T(8,128)(2,1)} %get-tuple-element.28, bf16[2048,1024]{1,0:T(8,128)(2,1)} %all-gather.7.cloned.1.call-done), kind=kOutput, calls=%fused_computation.69 | convolution fusion | flops 6462898176 | bytes 13631488 | tf_op jit(solution)/shard_map/rd,rkc->dkc/dot_general | solution.py:146
  585.5 34.8 %psum.50 = bf16[3,512]{1,0:T(4,128)(2,1)S(1)} all-reduce(bf16[3,512]{1,0:T(4,128)(2,1)S(1)} %pad_maximum_fusion.5), channel_id=1, replica_groups=mesh['dp'=16,'tensor'=2] {'dp'}, use_global_device_ids=true, to_apply=%region_15.16 | all-reduce | flops 1536 | bytes 6144 | tf_op jit(solution)/shard_map/psum | solution.py:170
  620.9 181.1 %all-reduce.6.cloned.1.call-done = (bf16[512,1024]{1,0:T(8,128)(2,1)}, bf16[1024,2304]{1,0:T(8,128)(2,1)}, bf16[1024,2304]{1,0:T(8,128)(2,1)}, bf16[2304,1024]{1,0:T(8,128)(2,1)}) async-done(((bf16[512,1024]{1,0:T(8,128)(2,1)}, bf16[1024,2304]{1,0:T(8,128)(2,1)}, bf16[1024,2304]{1,0:T(8,128)(2,1)}, bf16[2304,1024]{1,0:T(8,128)(2,1)}), (bf16[512,1024]{1,0:T(8,128)(2,1)}, bf16[1024,2304]{1,0:T(8,128)(2,1)}, ...) | async-done | bytes 15204368 | tf_op jit(solution)/shard_map/psum | solution.py:171
  821.3 37.1 %reduce-scatter.11.cloned.1.call-done = bf16[1024,1024]{1,0:T(8,128)(2,1)} async-done(((bf16[2048,1024]{1,0:T(8,128)(2,1)}), bf16[1024,1024]{1,0:T(8,128)(2,1)}) %reduce-scatter.11.cloned.1.call-update) | async-done | bytes 2097168 | tf_op jit(solution)/shard_map/reduce_scatter | solution.py:149
  861.7 40.7 %all-reduce.2 = (f32[1024]{0:T(1024)}, f32[1024]{0:T(1024)}) all-reduce(f32[1024]{0:T(1024)S(1)} %get-tuple-element.14, f32[1024]{0:T(1024)S(1)} %get-tuple-element.12), channel_id=1, replica_groups=mesh['dp'=16,'tensor'=2] {'dp','tensor'}, use_global_device_ids=true, to_apply=%region_10.11 | all-reduce | flops 2048 | bytes 16384 | tf_op jit(solution)/shard_map/psum | solution.py:176
  907.1 200.9 %all-gather.15.cloned.1.call-done = bf16[16384,3,512]{2,0,1:T(8,128)(2,1)} async-done(((bf16[1024,3,512]{2,0,1:T(8,128)(2,1)}), bf16[16384,3,512]{2,0,1:T(8,128)(2,1)}) %all-gather.15.cloned.1.call-update) | async-done | bytes 50331664 | tf_op jit(solution)/shard_map/all_gather | solution.py:167
  1108.0 18.3 %reduce_sum.98 = bf16[1024,3,512]{2,0,1:T(8,128)(2,1)} reduce(bf16[16,1024,3,512]{3,1,0,2:T(8,128)(2,1)} %bitcast.78, bf16[]{:T(256)} %constant.49.clone.1), dimensions={0}, to_apply=%region_11.12 | reduce | flops 23592960 | bytes 53477376 | tf_op jit(solution)/shard_map/reduce_sum | solution.py:167
  (143 shorter events, 137.7 us)
Async XLA Ops:
  7.2 90.6 %copy-start = (bf16[512,1024]{1,0:T(8,128)(2,1)S(1)}, bf16[512,1024]{1,0:T(8,128)(2,1)}, u32[]{:S(2)}) copy-start(bf16[512,1024]{1,0:T(8,128)(2,1)} %param.15) | copy-start | bytes 3145732
  7.2 65.9 %all-gather.7.cloned.1.call-start = ((), (), s32[]{:S(2)}) async-start(), calls=%async_computation.4 | async-start | bytes 6291456 | tf_op jit(solution)/shard_map/all_gather | solution.py:43
  13.5 143.1 %reduce-scatter.5.cloned.1.call-start = ((), (), s32[]{:S(2)}) async-start(), calls=%async_computation.5 | async-start | bytes 6291456 | tf_op jit(solution)/shard_map/reduce_scatter | solution.py:61
  18.2 67.8 %copy-start.17 = (f32[1,512]{1,0:T(1,128)}, f32[1,512]{1,0:T(1,128)S(1)}, u32[]{:S(2)}) copy-start(f32[1,512]{1,0:T(1,128)S(1)} %get-tuple-element.35) | copy-start | bytes 6148
  18.2 67.8 %copy-start.19 = (f32[1,512]{1,0:T(1,128)}, f32[1,512]{1,0:T(1,128)S(1)}, u32[]{:S(2)}) copy-start(f32[1,512]{1,0:T(1,128)S(1)} %get-tuple-element.36) | copy-start | bytes 6148
  18.2 67.8 %copy-start.21 = (f32[1,512]{1,0:T(1,128)}, f32[1,512]{1,0:T(1,128)S(1)}, u32[]{:S(2)}) copy-start(f32[1,512]{1,0:T(1,128)S(1)} %get-tuple-element.37) | copy-start | bytes 6148
  102.1 54.5 %copy-start.1 = (bf16[1024,1024]{1,0:T(8,128)(2,1)S(1)}, bf16[1024,1024]{1,0:T(8,128)(2,1)}, u32[]{:S(2)}) copy-start(bf16[1024,1024]{1,0:T(8,128)(2,1)} %param.11) | copy-start | bytes 6291460
  102.1 58.2 %copy-start.12 = (f32[1024]{0:T(1024)S(1)}, f32[1024]{0:T(1024)}, u32[]{:S(2)}) copy-start(f32[1024]{0:T(1024)} %param.16) | copy-start | bytes 12292
  102.1 117.2 %all-gather.9.cloned.1.call-start = ((), (), s32[]{:S(2)}) async-start(), calls=%async_computation.6 | async-start | bytes 6291456 | tf_op jit(solution)/shard_map/all_gather | solution.py:68
  162.4 115.7 %all-gather.11.cloned.1.call-start = ((), (), s32[]{:S(2)}) async-start(), calls=%async_computation.8 | async-start | bytes 6291456 | tf_op jit(solution)/shard_map/all_gather | solution.py:93
  162.6 73.6 %copy-start.15 = (f32[1024]{0:T(1024)}, f32[1024]{0:T(1024)S(1)}, u32[]{:S(2)}) copy-start(f32[1024]{0:T(1024)S(1)} %convert_element_type.123) | copy-start | bytes 12292
  165.9 232.9 %reduce-scatter.9.cloned.1.call-start = ((), (), s32[]{:S(2)}) async-start(), calls=%async_computation.9 | async-start | bytes 6291456 | tf_op jit(solution)/shard_map/reduce_scatter | solution.py:109
  344.4 110.9 %reduce-scatter.7.cloned.1.call-start = ((), (), s32[]{:S(2)}) async-start(), calls=%async_computation.7 | async-start | bytes 6291456 | tf_op jit(solution)/shard_map/reduce_scatter | solution.py:76
  360.1 38.8 %copy-start.11 = (f32[1024]{0:T(1024)S(1)}, f32[1024]{0:T(1024)}, u32[]{:S(2)}) copy-start(f32[1024]{0:T(1024)} %copy-done.10) | copy-start | bytes 12292
  360.1 38.8 %copy-start.13 = (f32[1024]{0:T(1024)S(1)}, f32[1024]{0:T(1024)}, u32[]{:S(2)}) copy-start(f32[1024]{0:T(1024)} %param.16) | copy-start | bytes 12292
  360.1 95.2 %copy-start.16 = (f32[1024]{0:T(1024)S(1)}, f32[1024]{0:T(1024)}, u32[]{:S(2)}) copy-start(f32[1024]{0:T(1024)} %copy-done.15) | copy-start | bytes 12292
  360.1 95.2 %copy-start.24 = (f32[1024]{0:T(1024)S(1)}, f32[1024]{0:T(1024)}, u32[]{:S(2)}) copy-start(f32[1024]{0:T(1024)} %get-tuple-element.33) | copy-start | bytes 12292
  360.1 158.9 %all-gather.13.cloned.1.call-start = ((), (), s32[]{:S(2)}) async-start(), calls=%async_computation.10 | async-start | bytes 6291456 | tf_op jit(solution)/shard_map/all_gather | solution.py:120
  462.1 339.9 %all-reduce.6.cloned.1.call-start = ((), (), s32[]{:S(2)}) async-start(), calls=%async_computation.13 | async-start | bytes 30408704 | tf_op jit(solution)/shard_map/psum | solution.py:171
  525.3 333.2 %reduce-scatter.11.cloned.1.call-start = ((), (), s32[]{:S(2)}) async-start(), calls=%async_computation.11 | async-start | bytes 6291456 | tf_op jit(solution)/shard_map/reduce_scatter | solution.py:149
  567.0 541.0 %all-gather.15.cloned.1.call-start = ((), (), s32[]{:S(2)}) async-start(), calls=%async_computation.12 | async-start | bytes 53477376 | tf_op jit(solution)/shard_map/all_gather | solution.py:167
  816.4 42.0 %copy-start.9 = (f32[1024]{0:T(1024)S(1)}, f32[1024]{0:T(1024)}, u32[]{:S(2)}) copy-start(f32[1024]{0:T(1024)} %copy-done.8) | copy-start | bytes 12292
  816.4 42.0 %copy-start.14 = (f32[1024]{0:T(1024)S(1)}, f32[1024]{0:T(1024)}, u32[]{:S(2)}) copy-start(f32[1024]{0:T(1024)} %param.12) | copy-start | bytes 12292
  821.3 81.0 %copy-start.23 = (f32[1024]{0:T(1024)S(1)}, f32[1024]{0:T(1024)}, u32[]{:S(2)}) copy-start(f32[1024]{0:T(1024)} %get-tuple-element.31) | copy-start | bytes 12292
  (26 other events, 331.3 us)
Sparse Core Ops, SparseCore 0:
  13.6 59.4 all-gather.6
  102.2 54.2 reduce-scatter.4
  162.5 56.7 all-gather.8
  221.3 56.7 all-gather.10
  344.5 54.3 reduce-scatter.8
  401.0 54.2 reduce-scatter.6
  462.2 56.7 all-gather.12
  525.4 276.5 all-reduce.5
  804.4 54.0 reduce-scatter.10
  859.8 248.1 all-gather.14
